TPU v7x, 32 devices: a whole 2x2x4 slice. The times are simulated.
32 devices in a mesh: groups: 2 (over y), probe: 4 (over z), depth: 2 (over x), tile: 2 (over core).
Axes of the slice: x: 2, y: 2, z: 4, core: 2. Of those that a mesh axis runs over, the one named last changes fastest.
Arguments:
- stored_waves: bfloat16 [2, 16, 2, 256, 256], P('depth', ('groups', 'probe', 'tile')), parts along dimension 1, may hold values from -6 to 6
- transmission: bfloat16 [2, 16, 2, 256, 256], P('depth', ('groups', 'probe', 'tile')), parts along dimension 1
- residual: float32 [16, 2, 256, 256], P(('groups', 'probe', 'tile')), parts along dimension 0, may hold values from -0.6 to 0.6
- offsets: int32 [16, 2], P('groups'), parts along dimension 0, may hold values from 0 to 256
- slot_position: int32 [16], P(('groups', 'probe', 'tile')), parts along dimension 0, may hold values from 0 to 7, each once
Outputs:
- object_gradient: float32 [4, 2, 512, 512], P('groups', 'depth', 'probe', 'tile'), parts along dimension 0
There are 2 independent parts, one for each index of `groups`. A program takes and returns all parts, laid end to end along the dimension named above; each array names one. Nothing has to cross between parts.
Inputs may be any that keep to these rules, and one draw needn't show every extreme that they name: `slot_position`: every scan position is held by exactly one slot.
All inputs are finite; a program needn't handle non-finite values.
Results may differ from a plain program's by a relative error of at most 0.0032.
Values may be sent and summed in bfloat16 or wider, within the bound.
A program may use at most 64 MiB of HBM per device.

v0:
```python
import math

import jax
import jax.numpy as jnp
from jax import lax
from jax.sharding import PartitionSpec as P

OBJ = 512


def from_behind(value, axis, steps):
    count = lax.axis_size(axis)
    leading, last = (max(0, -steps), min(count, count - steps))
    return lax.ppermute(value, axis, [(source, source + steps) for source in range(leading, last)])


def dft_tables(side_length):
    counter = lax.iota(jnp.int32, side_length)
    turns = counter[:, None] * counter[None, :] % side_length
    angle = turns.astype(jnp.float32) * (2.0 * math.pi / side_length)
    frequency = ((counter + side_length // 2) % side_length - side_length // 2).astype(jnp.float32)
    phase_angle = (
        0.5
        * (frequency[:, None] * frequency[:, None] + frequency[None, :] * frequency[None, :])
        / side_length
    )
    return (jnp.cos(angle), jnp.sin(angle), jnp.cos(phase_angle), jnp.sin(phase_angle))


def left_apply(matrix, field):
    return jnp.einsum("kn,pnm->pkm", matrix, field, precision=lax.Precision.HIGHEST)


def right_apply(matrix, field):
    return jnp.einsum("pnm,mk->pnk", field, matrix, precision=lax.Precision.HIGHEST)


def complex_left(tables, direction_sign, real_part, imag_part):
    cosine = tables[0]
    sine_table = tables[1]
    return (
        left_apply(cosine, real_part) - direction_sign * left_apply(sine_table, imag_part),
        left_apply(cosine, imag_part) + direction_sign * left_apply(sine_table, real_part),
    )


def complex_right(tables, direction_sign, real_part, imag_part):
    cosine = tables[0]
    sine_table = tables[1]
    return (
        right_apply(cosine, real_part) - direction_sign * right_apply(sine_table, imag_part),
        right_apply(cosine, imag_part) + direction_sign * right_apply(sine_table, real_part),
    )


def back_propagate(tables, real_part, imag_part):
    side_length = real_part.shape[-1]
    spec_real, spec_imag = complex_left(tables, -1.0, real_part, imag_part)
    spec_real, spec_imag = complex_right(tables, -1.0, spec_real, spec_imag)
    turn_real = spec_real * tables[2] - spec_imag * tables[3]
    turn_imag = spec_real * tables[3] + spec_imag * tables[2]
    back_real, back_imag = complex_left(tables, 1.0, turn_real, turn_imag)
    back_real, back_imag = complex_right(tables, 1.0, back_real, back_imag)
    inverse_area = 1.0 / (side_length * side_length)
    return (back_real * inverse_area, back_imag * inverse_area)


def per_device(stored_waves, transmission, residual, offsets, slot_position):
    slot_count = stored_waves.shape[1]
    side_length = stored_waves.shape[-1]
    depth_count = lax.axis_size("depth")
    depth_index = lax.axis_index("depth")
    is_top = depth_index == depth_count - 1
    tables = dft_tables(side_length)
    every_position = lax.iota(jnp.int32, offsets.shape[0])
    matches = (slot_position[:, None] == every_position[None, :]).astype(jnp.int32)
    own_offsets = jnp.sum(matches[:, :, None] * offsets[None, :, :], axis=1)
    slice_waves = stored_waves[0]
    slice_layers = transmission[0]
    empty_region = jnp.zeros((2, 1, OBJ, OBJ), jnp.float32)

    def advance(incoming, region, front_size):

        def start_top():
            return (residual[:, 0], residual[:, 1])

        def start_below():
            return back_propagate(
                tables, incoming[:, 0].astype(jnp.float32), incoming[:, 1].astype(jnp.float32)
            )

        adjoint_real, adjoint_imag = lax.cond(is_top, start_top, start_below)
        waves_here = slice_waves.astype(jnp.float32)
        layers_here = slice_layers.astype(jnp.float32)
        grad_real = waves_here[:, 0] * adjoint_real + waves_here[:, 1] * adjoint_imag
        grad_imag = waves_here[:, 0] * adjoint_imag - waves_here[:, 1] * adjoint_real
        handed = jnp.stack(
            [
                layers_here[:, 0] * adjoint_real + layers_here[:, 1] * adjoint_imag,
                layers_here[:, 0] * adjoint_imag - layers_here[:, 1] * adjoint_real,
            ],
            1,
        ).astype(jnp.bfloat16)
        gradient = jnp.stack([grad_real, grad_imag], 0)

        def add_patch(number, region):
            patch_value = lax.dynamic_index_in_dim(gradient, number, 1, keepdims=True)
            anchor = jnp.int32(0)
            corner = (anchor, anchor, own_offsets[number, 0], own_offsets[number, 1])
            current = lax.dynamic_slice(region, corner, (2, 1, side_length, side_length))
            return lax.dynamic_update_slice(region, current + patch_value, corner)

        return (handed, lax.fori_loop(0, front_size, add_patch, region))

    front_size = slot_count

    def handoff(handed):
        return from_behind(handed, "depth", -1)

    resting = jnp.zeros((front_size, 2, side_length, side_length), jnp.bfloat16)

    def one_turn(turn, incoming, region):
        front = (turn - (depth_count - 1 - depth_index)) * front_size
        active = (front >= 0) & (front + front_size <= slot_count)
        return lax.cond(
            active, lambda: advance(incoming, region, front_size), lambda: (resting, region)
        )

    start_state = one_turn(0, resting, empty_region)

    def loop_body(turn, carry):
        return one_turn(turn, handoff(carry[0]), carry[1])

    final_state = lax.fori_loop(1, depth_count, loop_body, start_state)
    region = final_state[1]
    strips = lax.psum_scatter(region, "probe", scatter_dimension=2, tiled=True)
    return lax.psum_scatter(strips, "tile", scatter_dimension=3, tiled=True)


def solution(mesh):
    return jax.shard_map(
        per_device,
        mesh=mesh,
        in_specs=(
            P("depth", ("groups", "probe", "tile"), None, None, None),
            P("depth", ("groups", "probe", "tile"), None, None, None),
            P(("groups", "probe", "tile"), None, None, None),
            P("groups", None),
            P(("groups", "probe", "tile")),
        ),
        out_specs=P("groups", "depth", "probe", "tile"),
        check_vma=False,
    )
```

profile of v0, /device:TPU:0, one launch (start us, length us, event | category | flops | bytes accessed | tf_op | source)
XLA Modules:
  0.0 116.7 jit_solution(14352994091525498350)
XLA Ops:
  6.5 0.0 reduce-scatter.3.cloned.1.call-start
  6.5 1.0 fusion.46
  8.2 1.0 fusion.41
  9.3 0.8 multiply_reduce_fusion.2
  10.1 1.6 %conditional.4 = (bf16[1,2,256,256]{3,2,1,0:T(8,128)(2,1)S(1)}, f32[2,1,512,512]{3,2,1,0:T(8,128)}) conditional(s32[]{:T(128)} %convert_element_type.146, () %tuple.50, (bf16[1,1,2,256,256]{4,3,2,1,0:T(8,128)(2,1)}, pred[]{:T(512)}, f32[256,256]{1,0:T(8,128)S(1)}, f32[256,256]{1,0:T(8,128)S(1)}, f32[256,256]{1,0:T(8,128)S(1)}, ...), branch_computations={%region_1.2_spmd, %region_2.7_spmd} | conditional | flops 2418671872 | bytes 22817092 | solution.py:125
  10.1 1.6 %broadcast_in_dim.4 = f32[2,1,512,512]{3,2,1,0:T(8,128)} broadcast(f32[]{:T(128)} %constant.80.clone), dimensions={} | broadcast | bytes 2097156 | tf_op jit(solution)/shard_map/broadcast_in_dim | solution.py:80
  11.7 1.3 %collective-permute-start = (bf16[1,2,256,256]{3,2,1,0:T(8,128)(2,1)S(1)}, bf16[1,2,256,256]{3,2,1,0:T(8,128)(2,1)S(1)}, u32[]{:S(2)}, u32[]{:S(2)}) collective-permute-start(bf16[1,2,256,256]{3,2,1,0:T(8,128)(2,1)S(1)} %get-tuple-element.329), channel_id=1, source_target_pairs={{2,0},{3,1},{6,4},{7,5},{10,8},{11,9},{14,12},{15,13},{18,16},{19,... | collective-permute-start | bytes 786440 | tf_op jit(solution)/shard_map/while/body/eval_jaxpr/ppermute | solution.py:14
  13.0 20.5 %collective-permute-done = bf16[1,2,256,256]{3,2,1,0:T(8,128)(2,1)S(1)} collective-permute-done((bf16[1,2,256,256]{3,2,1,0:T(8,128)(2,1)S(1)}, bf16[1,2,256,256]{3,2,1,0:T(8,128)(2,1)S(1)}, u32[]{:S(2)}, u32[]{:S(2)}) %collective-permute-start) | collective-permute-done | bytes 262176 | tf_op jit(solution)/shard_map/while/body/eval_jaxpr/ppermute | solution.py:14
  33.5 21.5 %conditional.5 = (f32[2,1,512,512]{3,2,1,0:T(8,128)}) conditional(s32[]{:T(128)} %convert_element_type.145, f32[2,1,512,512]{3,2,1,0:T(8,128)} %get-tuple-element.328, (s32[1,2]{1,0:T(1,128)S(1)}, f32[2,1,512,512]{3,2,1,0:T(8,128)}, bf16[1,2,256,256]{3,2,1,0:T(8,128)(2,1)}, pred[]{:T(512)}, bf16[1,2,256,256]{3,2,1,0:T(8,128)(2,1)S(1)}, ...), branch_computations={%region_7.8_spmd, %region_8.11_spmd} | conditional | flops 3223322624 | bytes 21758268 | solution.py:125
  33.5 0.0 copy-start.1
  33.5 8.6 %conditional.1 = (f32[1,256,256]{2,1,0:T(8,128)S(1)}, f32[1,256,256]{2,1,0:T(8,128)S(1)}) conditional(s32[]{:T(128)} %convert_element_type.103, (bf16[1,2,256,256]{3,2,1,0:T(8,128)(2,1)S(1)}, f32[256,256]{1,0:T(8,128)S(1)}, f32[256,256]{1,0:T(8,128)S(1)}, f32[256,256]{1,0:T(8,128)S(1)}, f32[256,256]{1,0:T(8,128)S(1)}, ...), branch_computations={%region_9.9_spmd, %region_10.10_spmd} | conditional | flops 3222536192 | bytes 15728656 | solution.py:92
  33.5 0.3 fusion.32
  33.8 0.3 fusion.27
  34.2 0.6 fusion.54
  34.8 0.3 fusion.28
  35.1 0.3 fusion.25
  35.4 0.6 fusion.23
  36.0 0.6 fusion.55
  36.7 0.6 multiply_add_fusion.2
  37.3 0.6 fusion.58
  37.9 0.6 fusion.20
  38.5 0.6 fusion.56
  39.1 0.6 fusion.21
  39.7 0.6 fusion.57
  40.3 0.6 fusion.19
  40.9 0.6 fusion.59
  41.5 0.6 fusion.17
  42.1 0.6 fusion.53
  46.7 0.0 copy-done.1
  46.7 0.1 add_bitcast_fusion.1
  46.8 1.4 %maximum_add_fusion = f32[2,1,256,256]{3,2,1,0:T(8,128)S(1)} fusion(f32[1,1,256,256]{3,2,1,0:T(8,128)S(1)} %get-tuple-element.353, f32[1,1,256,256]{3,2,1,0:T(8,128)S(1)} %get-tuple-element.352, f32[2,1,512,512]{3,2,1,0:T(8,128)} %get-tuple-element.298, s32[]{:T(128)S(6)} %select_n.86, s32[]{:T(128)S(6)} %select_n.87), kind=kLoop, calls=%fused_computation.75 | loop fusion | flops 262144 | bytes 1572872 | tf_op jit(solution)/shard_map/while/body/eval_jaxpr/cond/branch_1_fun/while/body/eval_jaxpr/add | solution.py:111
  48.2 6.8 %dynamic_update_slice.9 = f32[2,1,512,512]{3,2,1,0:T(8,128)} dynamic-update-slice(f32[2,1,512,512]{3,2,1,0:T(8,128)} %get-tuple-element.298, f32[2,1,256,256]{3,2,1,0:T(8,128)S(1)} %maximum_add_fusion, s32[]{:T(128)} %constant.89.clone, s32[]{:T(128)} %constant.89.clone, s32[]{:T(128)S(6)} %select_n.86, s32[]{:T(128)S(6)} %select_n.87) | dynamic-update-slice | bytes 1048580 | tf_op jit(solution)/shard_map/while/body/eval_jaxpr/cond/branch_1_fun/while/body/eval_jaxpr/dynamic_update_slice | solution.py:111
  55.0 0.0 reduce-scatter.3.cloned.1.call-update
  55.0 0.0 reduce-scatter.5.cloned.1.call-start
  55.0 45.2 %reduce-scatter.3.cloned.1.call-done = f32[2,1,128,512]{3,2,1,0:T(8,128)} async-done(((f32[2,1,512,512]{3,2,1,0:T(8,128)}), f32[2,1,128,512]{3,2,1,0:T(8,128)}) %reduce-scatter.3.cloned.1.call-update) | async-done | bytes 524304 | tf_op jit(solution)/shard_map/reduce_scatter | solution.py:136
  100.3 0.0 reduce-scatter.5.cloned.1.call-update
  100.3 9.6 %reduce-scatter.5.cloned.1.call-done = f32[2,1,128,256]{3,2,1,0:T(8,128)} async-done(((f32[2,1,128,512]{3,2,1,0:T(8,128)}), f32[2,1,128,256]{3,2,1,0:T(8,128)}) %reduce-scatter.5.cloned.1.call-update) | async-done | bytes 262160 | tf_op jit(solution)/shard_map/reduce_scatter | solution.py:137
  (4 shorter events, 0.1 us)
Async XLA Ops:
  6.5 93.7 %reduce-scatter.3.cloned.1.call-start = ((), (), s32[]{:S(2)}) async-start(), calls=%async_computation.2 | async-start | bytes 2621440 | tf_op jit(solution)/shard_map/reduce_scatter | solution.py:136
  11.7 21.8 %collective-permute-start = (bf16[1,2,256,256]{3,2,1,0:T(8,128)(2,1)S(1)}, bf16[1,2,256,256]{3,2,1,0:T(8,128)(2,1)S(1)}, u32[]{:S(2)}, u32[]{:S(2)}) collective-permute-start(bf16[1,2,256,256]{3,2,1,0:T(8,128)(2,1)S(1)} %get-tuple-element.329), channel_id=1, source_target_pairs={{2,0},{3,1},{6,4},{7,5},{10,8},{11,9},{14,12},{15,13},{18,16},{19,... | collective-permute-start | bytes 786440 | tf_op jit(solution)/shard_map/while/body/eval_jaxpr/ppermute | solution.py:14
  33.5 13.2 %copy-start.1 = (bf16[1,2,256,256]{3,2,1,0:T(8,128)(2,1)S(1)}, bf16[1,2,256,256]{3,2,1,0:T(8,128)(2,1)}, u32[]{:S(2)}) copy-start(bf16[1,2,256,256]{3,2,1,0:T(8,128)(2,1)} %get-tuple-element.300) | copy-start | bytes 786436 | tf_op jit(solution)/shard_map/while/body/eval_jaxpr/cond
  55.0 54.9 %reduce-scatter.5.cloned.1.call-start = ((), (), s32[]{:S(2)}) async-start(), calls=%async_computation.3 | async-start | bytes 786432 | tf_op jit(solution)/shard_map/reduce_scatter | solution.py:137
Sparse Core Ops, SparseCore 0:
  55.1 45.1 reduce-scatter.2
  102.6 7.2 reduce-scatter.4
where the time goes:
time: 117 us
  waiting for transfers between devices  75.4 us (64%)
  between operations  14.1 us (12%)
  local copies, waits for them, and re-layouts  8.99 us (8%)
  matrix products  8.52 us (7%)
  other arithmetic  4.32 us (4%)
  loops' own time  4.1 us (4%)
  starting transfers between devices  1.32 us (1%)
    reduce_scatter x1, waiting for transfers between devices, per_device(): strips = lax.psum_scatter(region, 'probe', scatter_dimension=2, tiled=True)  45.2 us
    ppermute x1, waiting for transfers between devices, from_behind(): lax.ppermute(value, axis, [(source, source + steps) for source in range(l...  20.5 us
    reduce_scatter x1, waiting for transfers between devices, per_device(): return lax.psum_scatter(strips, 'tile', scatter_dimension=3, tiled=True)  9.61 us
    dynamic_update_slice x1, local copies, waits for them, and re-layouts, add_patch(): return lax.dynamic_update_slice(region, current + patch_value, corner)  6.78 us
    dot_general x8, matrix products, right_apply(): jnp.einsum('pnm,mk->pnk', field, matrix, precision=lax.Precision.HIGHEST)  4.82 us
    another operation x2, loops' own time, one_turn(): lax.cond(active, lambda: advance(incoming, region, front_size), lambda: (...  3.99 us
    dot_general x8, matrix products, left_apply(): jnp.einsum('kn,pnm->pkm', matrix, field, precision=lax.Precision.HIGHEST)  3.71 us
  transfers between devices with their start and end apart: 3, of which 3 were waited for; matrix products, arithmetic and copies ran while one was open for 0% of the time, Pallas kernels for 0%

commit v1 on v0

v1 whole, which is shorter than its diff:
```python
import functools

import jax
import jax.numpy as jnp
import ml_dtypes
import numpy as np
from jax import lax
from jax.experimental import pallas as pl
from jax.experimental.pallas import tpu as pltpu
from jax.sharding import PartitionSpec as P

OBJ = 512
CHUNKS = 4
MESH = pl.DeviceIdType.MESH
F32 = jnp.float32
BF16 = jnp.bfloat16


def propagator(side):
    counter = np.arange(side)
    frequency = (counter + side // 2) % side - side // 2
    chirp = np.exp(0.5j * frequency.astype(np.float64) ** 2 / side)
    column = np.fft.ifft(chirp)
    matrix = column[(counter[:, None] - counter[None, :]) % side]
    parts = np.stack([matrix.real, matrix.imag])
    high = parts.astype(ml_dtypes.bfloat16)
    low = (parts - high.astype(np.float64)).astype(ml_dtypes.bfloat16)
    return high, low


def dot(a, b):
    return jnp.dot(a, b, preferred_element_type=F32)


def split(value):
    high = value.astype(BF16)
    return high, (value - high.astype(F32)).astype(BF16)


def conj_times(layer_real, layer_imag, real, imag):
    return (
        layer_real * real + layer_imag * imag,
        layer_real * imag - layer_imag * real,
    )


def flip(index, mask, count):
    result, bit = 0, 1
    while bit < count:
        result = result + ((index // bit + (mask // bit) % 2) % 2) * bit
        bit *= 2
    return result


def kernel(
    depth_count,
    probe_count,
    waves,
    layers,
    residual,
    offsets,
    slot,
    high,
    low,
    out,
    hand_out,
    hand_in,
    turned_high,
    turned_low,
    grads,
    corners,
    strips_out,
    strips_in,
    hand_sems,
    grad_sems,
    corner_sems,
    strip_sems,
):
    side = waves.shape[-1]
    rows, columns = out.shape[2], out.shape[3]
    step = side // CHUNKS
    depth = lax.axis_index("depth")
    probe = lax.axis_index("probe")
    tile = lax.axis_index("tile")
    is_top = depth == depth_count - 1
    has_below = depth > 0

    barrier = pltpu.get_barrier_semaphore()
    for mask in range(1, probe_count):
        pl.semaphore_signal(
            barrier, inc=1, device_id={"probe": flip(probe, mask, probe_count)}, device_id_type=MESH
        )
    pl.semaphore_signal(barrier, inc=1, device_id={"tile": 1 - tile}, device_id_type=MESH)

    @pl.when(depth < depth_count - 1)
    def _():
        pl.semaphore_signal(barrier, inc=1, device_id={"depth": depth + 1}, device_id_type=MESH)

    own_slot = slot[0]
    top_row = offsets[own_slot, 0]
    left_column = offsets[own_slot, 1]
    corners[0, 0:8, :] = jnp.full((8, side), top_row, jnp.int32)
    corners[0, 8:16, :] = jnp.full((8, side), left_column, jnp.int32)

    @pl.when(has_below)
    def _():
        pl.semaphore_wait(barrier, probe_count + 1)

    @pl.when(jnp.logical_not(has_below))
    def _():
        pl.semaphore_wait(barrier, probe_count)

    corner_copy = pltpu.make_async_remote_copy(
        src_ref=corners.at[0],
        dst_ref=corners.at[1],
        send_sem=corner_sems.at[0],
        recv_sem=corner_sems.at[1],
        device_id={"tile": 1 - tile},
        device_id_type=MESH,
    )
    corner_copy.start()

    def hand_copy(part):
        window = pl.ds(part * step, step)
        return pltpu.make_async_remote_copy(
            src_ref=hand_out.at[:, window, :],
            dst_ref=hand_in.at[:, window, :],
            send_sem=hand_sems.at[0, part],
            recv_sem=hand_sems.at[1, part],
            device_id={"depth": depth - 1},
            device_id_type=MESH,
        )

    def grad_copy(part):
        window = pl.ds(part * step, step)
        return pltpu.make_async_remote_copy(
            src_ref=grads.at[0, :, window, :],
            dst_ref=grads.at[1, :, window, :],
            send_sem=grad_sems.at[0, part],
            recv_sem=grad_sems.at[1, part],
            device_id={"tile": 1 - tile},
            device_id_type=MESH,
        )

    def hand_down(part, real, imag):
        window = pl.ds(part * step, step)
        handed = conj_times(
            layers[0, 0, 0, window, :].astype(F32), layers[0, 0, 1, window, :].astype(F32), real, imag
        )
        hand_out[0, window, :] = handed[0].astype(BF16)
        hand_out[1, window, :] = handed[1].astype(BF16)
        hand_copy(part).start()

    def give_gradient(part, real, imag):
        window = pl.ds(part * step, step)
        gradient = conj_times(
            waves[0, 0, 0, window, :].astype(F32), waves[0, 0, 1, window, :].astype(F32), real, imag
        )
        grads[0, 0, window, :] = gradient[0].astype(BF16)
        grads[0, 1, window, :] = gradient[1].astype(BF16)
        grad_copy(part).start()

    @pl.when(is_top)
    def _():
        if depth_count > 1:
            for part in range(CHUNKS):
                window = pl.ds(part * step, step)
                hand_down(part, residual[0, 0, window, :], residual[0, 1, window, :])
        for part in range(CHUNKS):
            window = pl.ds(part * step, step)
            give_gradient(part, residual[0, 0, window, :], residual[0, 1, window, :])

    if depth_count > 1:

        @pl.when(depth < depth_count - 1)
        def _():
            for part in range(CHUNKS):
                window = pl.ds(part * step, step)
                hand_copy(part).wait_recv()
                real, imag = hand_in[0, window, :], hand_in[1, window, :]

                def times(index):
                    return (
                        dot(real, high[index]) + dot(real, low[index]),
                        dot(imag, high[index]) + dot(imag, low[index]),
                    )

                real_cos, imag_cos = times(0)
                real_sin, imag_sin = times(1)
                for index, value in enumerate((real_cos - imag_sin, real_sin + imag_cos)):
                    turned_high[index, window, :], turned_low[index, window, :] = split(value)

            for part in range(CHUNKS):
                window = pl.ds(part * step, step)

                def from_left(table, field):
                    return (
                        dot(high[table, window, :], turned_high[field])
                        + dot(low[table, window, :], turned_high[field])
                        + dot(high[table, window, :], turned_low[field])
                    )

                real = from_left(0, 0) - from_left(1, 1)
                imag = from_left(0, 1) + from_left(1, 0)
                if depth_count > 2:

                    @pl.when(has_below)
                    def _():
                        hand_down(part, real, imag)

                give_gradient(part, real, imag)

    row_index = lax.broadcasted_iota(jnp.int32, (side, columns), 0)
    column_index = lax.broadcasted_iota(jnp.int32, (side, columns), 1) + tile * columns

    def onehot(match):
        return jnp.where(match, 1.0, 0.0).astype(BF16)

    own_columns = onehot(column_index - row_index == left_column)
    placed = [[dot(grads[0, c], own_columns).astype(BF16)] for c in range(2)]

    corner_copy.wait_recv()
    for part in range(CHUNKS):
        grad_copy(part).wait_recv()
    peer_row = corners[1, 0:1, :]
    peer_columns = onehot(column_index - row_index == corners[1, 8:9, 0:columns])
    for c in range(2):
        placed[c].append(dot(grads[1, c], peer_columns).astype(BF16))

    strip_row = lax.broadcasted_iota(jnp.int32, (rows, side), 0)
    patch_row = lax.broadcasted_iota(jnp.int32, (rows, side), 1)
    distance = strip_row - patch_row

    def strip(owner):
        shifted = distance + owner * rows
        own_rows = onehot(shifted == top_row)
        peer_rows = onehot(shifted == peer_row)
        return [dot(own_rows, placed[c][0]) + dot(peer_rows, placed[c][1]) for c in range(2)]

    def strip_copy(mask):
        return pltpu.make_async_remote_copy(
            src_ref=strips_out.at[mask - 1],
            dst_ref=strips_in.at[mask - 1],
            send_sem=strip_sems.at[0, mask - 1],
            recv_sem=strip_sems.at[1, mask - 1],
            device_id={"probe": flip(probe, mask, probe_count)},
            device_id_type=MESH,
        )

    for mask in range(probe_count - 1, 0, -1):
        real, imag = strip(flip(probe, mask, probe_count))
        strips_out[mask - 1, 0] = real.astype(BF16)
        strips_out[mask - 1, 1] = imag.astype(BF16)
        strip_copy(mask).start()
    total = strip(probe)
    for c in range(2):
        out[c, 0] = total[c]
    for mask in range(1, probe_count):
        strip_copy(mask).wait_recv()
        for c in range(2):
            out[c, 0] += strips_in[mask - 1, c].astype(F32)

    corner_copy.wait_send()
    for part in range(CHUNKS):
        grad_copy(part).wait_send()
    for mask in range(1, probe_count):
        strip_copy(mask).wait_send()

    @pl.when(has_below)
    def _():
        for part in range(CHUNKS):
            hand_copy(part).wait_send()


def per_device(depth_count, probe_count, tile_count, waves, layers, residual, offsets, slot):
    side = waves.shape[-1]
    high, low = propagator(side)
    rows, columns = OBJ // probe_count, OBJ // tile_count
    vmem = pl.BlockSpec(memory_space=pltpu.VMEM)
    smem = pl.BlockSpec(memory_space=pltpu.SMEM)
    return pl.pallas_call(
        functools.partial(kernel, depth_count, probe_count),
        out_shape=jax.ShapeDtypeStruct((2, 1, rows, columns), F32),
        in_specs=[vmem, vmem, vmem, smem, smem, vmem, vmem],
        out_specs=vmem,
        scratch_shapes=[
            pltpu.VMEM((2, side, side), BF16),
            pltpu.VMEM((2, side, side), BF16),
            pltpu.VMEM((2, side, side), BF16),
            pltpu.VMEM((2, side, side), BF16),
            pltpu.VMEM((2, 2, side, side), BF16),
            pltpu.VMEM((2, 16, side), jnp.int32),
            pltpu.VMEM((probe_count - 1, 2, rows, columns), BF16),
            pltpu.VMEM((probe_count - 1, 2, rows, columns), BF16),
            pltpu.SemaphoreType.DMA((2, CHUNKS)),
            pltpu.SemaphoreType.DMA((2, CHUNKS)),
            pltpu.SemaphoreType.DMA((2,)),
            pltpu.SemaphoreType.DMA((2, probe_count - 1)),
        ],
        compiler_params=pltpu.CompilerParams(
            collective_id=0, has_side_effects=True, vmem_limit_bytes=32 * 1024 * 1024
        ),
    )(waves, layers, residual, offsets, slot, jnp.asarray(high), jnp.asarray(low))


def solution(mesh):
    return jax.shard_map(
        functools.partial(per_device, mesh.shape["depth"], mesh.shape["probe"], mesh.shape["tile"]),
        mesh=mesh,
        in_specs=(
            P("depth", ("groups", "probe", "tile"), None, None, None),
            P("depth", ("groups", "probe", "tile"), None, None, None),
            P(("groups", "probe", "tile"), None, None, None),
            P("groups", None),
            P(("groups", "probe", "tile")),
        ),
        out_specs=P("groups", "depth", "probe", "tile"),
        check_vma=False,
    )
```

time: 117 us -> 35.7 us (0.31)
  waiting for transfers between devices: 75.4 us -> 0 us
  Pallas kernels: 0 us -> 29.1 us
  between operations: 14.1 us -> 0.68 us
  matrix products: 8.52 us -> 0 us
  other arithmetic: 4.32 us -> 0 us
  loops' own time: 4.1 us -> 0 us
  local copies, waits for them, and re-layouts: 8.99 us -> 5.64 us
  starting transfers between devices: 1.32 us -> 0 us
    reduce_scatter x2 -> x0, waiting for transfers between devices: 54.9 us -> none  [the longest x1 45.2 us: per_device(): strips = lax.psum_scatter(region, 'probe', scatter_dimension=2, tiled=True)]
    pallas_call x0 -> x1, Pallas kernels: none -> 29.1 us  [per_device(): pl.pallas_call(functools.partial(kernel, depth_count, probe_count), out_s...]
    ppermute x1 -> x0, waiting for transfers between devices: 20.5 us -> none  [from_behind(): lax.ppermute(value, axis, [(source, source + steps) for source in range(l...]
    dot_general x16 -> x0, matrix products: 8.52 us -> none  [the longest x8 4.82 us: right_apply(): jnp.einsum('pnm,mk->pnk', field, matrix, precision=lax.Precision.HIGHEST)]
    dynamic_update_slice x1 -> x0, local copies, waits for them, and re-layouts: 6.78 us -> none  [add_patch(): return lax.dynamic_update_slice(region, current + patch_value, corner)]
    unnamed x0 -> x14, local copies, waits for them, and re-layouts: none -> 5.64 us
    another operation x3 -> x0, loops' own time: 4.1 us -> none  [the longest x2 3.99 us: one_turn(): lax.cond(active, lambda: advance(incoming, region, front_size), lambda: (...]
    sin x2 -> x0, other arithmetic: 2.04 us -> none  [the longest x1 1.03 us: dft_tables(): jnp.sin(angle)]
  transfers between devices with their start and end apart: 3 -> 0, of which waited for: 3 -> 0; matrix products, arithmetic and copies ran while one was open for 0% -> 0% of each run, Pallas kernels for 0% -> 0%
where the time goes in v1:
time: 35.7 us; the launch traced here: 35.4 us
  Pallas kernels  29.1 us (82%)
  local copies, waits for them, and re-layouts  5.64 us (16%)
  between operations  0.68 us (2%)
    pallas_call x1, Pallas kernels, per_device(): pl.pallas_call(functools.partial(kernel, depth_count, probe_count), out_s...  29.1 us
    unnamed x14, local copies, waits for them, and re-layouts  5.64 us

profile of v1, /device:TPU:0, one launch (start us, length us, event | category | flops | bytes accessed | tf_op | source)
XLA Modules:
  0.0 35.4 jit_solution(17807341467743262484)
XLA Ops:
  0.0 0.0 copy-start.5
  0.7 0.0 copy-done.5
  0.7 0.1 copy.8.offsets
  0.8 0.0 copy-start
  0.8 1.0 %copy-done = f32[1,2,256,256]{3,2,1,0:T(8,128)S(1)} copy-done((f32[1,2,256,256]{3,2,1,0:T(8,128)S(1)}, f32[1,2,256,256]{3,2,1,0:T(8,128)}, u32[]{:S(2)}) %copy-start) | copy-done | bytes 524312
  1.8 0.0 copy-start.1
  1.8 0.9 %copy-done.1 = bf16[1,1,2,256,256]{4,3,2,1,0:T(8,128)(2,1)S(1)} copy-done((bf16[1,1,2,256,256]{4,3,2,1,0:T(8,128)(2,1)S(1)}, bf16[1,1,2,256,256]{4,3,2,1,0:T(8,128)(2,1)}, u32[]{:S(2)}) %copy-start.1) | copy-done | bytes 262168
  2.8 0.0 copy-start.2
  2.8 0.9 %copy-done.2 = bf16[1,1,2,256,256]{4,3,2,1,0:T(8,128)(2,1)S(1)} copy-done((bf16[1,1,2,256,256]{4,3,2,1,0:T(8,128)(2,1)S(1)}, bf16[1,1,2,256,256]{4,3,2,1,0:T(8,128)(2,1)}, u32[]{:S(2)}) %copy-start.2) | copy-done | bytes 262168
  3.7 0.0 copy-start.3
  3.7 0.9 %copy-done.3 = bf16[2,256,256]{2,1,0:T(8,128)(2,1)S(1)} copy-done((bf16[2,256,256]{2,1,0:T(8,128)(2,1)S(1)}, bf16[2,256,256]{2,1,0:T(8,128)(2,1)}, u32[]{:S(2)}) %copy-start.3) | copy-done | bytes 262168
  4.7 0.0 copy-start.4
  4.7 0.9 %copy-done.4 = bf16[2,256,256]{2,1,0:T(8,128)(2,1)S(1)} copy-done((bf16[2,256,256]{2,1,0:T(8,128)(2,1)S(1)}, bf16[2,256,256]{2,1,0:T(8,128)(2,1)}, u32[]{:S(2)}) %copy-start.4) | copy-done | bytes 262168
  5.6 29.1 %shard_map.73 = f32[2,1,128,256]{3,2,1,0:T(8,128)S(1)} custom-call(bf16[1,1,2,256,256]{4,3,2,1,0:T(8,128)(2,1)S(1)} %copy-done.1, bf16[1,1,2,256,256]{4,3,2,1,0:T(8,128)(2,1)S(1)} %copy-done.2, f32[1,2,256,256]{3,2,1,0:T(8,128)S(1)} %copy-done, s32[8,2]{1,0:T(8,128)S(1)} %copy.8.offsets, s32[1]{0:T(128)S(6)} %copy.10.slot, ...), custom_call_target="tpu_custom_call" | custom-call | tf_op jit(solution)/shard_map/pallas_call | solution.py:281
  34.7 0.7 %copy.11 = f32[2,1,128,256]{3,2,1,0:T(8,128)} copy(f32[2,1,128,256]{3,2,1,0:T(8,128)S(1)} %shard_map.73) | data formatting | bytes 524288
Async XLA Ops:
  0.0 0.7 %copy-start.5 = (s32[8,2]{0,1:T(2,128)S(1)}, s32[8,2]{0,1:T(2,128)}, u32[]{:S(2)}) copy-start(s32[8,2]{0,1:T(2,128)} %param.10) | copy-start | bytes 196
  0.8 1.0 %copy-start = (f32[1,2,256,256]{3,2,1,0:T(8,128)S(1)}, f32[1,2,256,256]{3,2,1,0:T(8,128)}, u32[]{:S(2)}) copy-start(f32[1,2,256,256]{3,2,1,0:T(8,128)} %residual.1) | copy-start | bytes 1572868
  1.8 0.9 %copy-start.1 = (bf16[1,1,2,256,256]{4,3,2,1,0:T(8,128)(2,1)S(1)}, bf16[1,1,2,256,256]{4,3,2,1,0:T(8,128)(2,1)}, u32[]{:S(2)}) copy-start(bf16[1,1,2,256,256]{4,3,2,1,0:T(8,128)(2,1)} %waves.1) | copy-start | bytes 786436
  2.8 0.9 %copy-start.2 = (bf16[1,1,2,256,256]{4,3,2,1,0:T(8,128)(2,1)S(1)}, bf16[1,1,2,256,256]{4,3,2,1,0:T(8,128)(2,1)}, u32[]{:S(2)}) copy-start(bf16[1,1,2,256,256]{4,3,2,1,0:T(8,128)(2,1)} %layers.1) | copy-start | bytes 786436
  3.7 0.9 %copy-start.3 = (bf16[2,256,256]{2,1,0:T(8,128)(2,1)S(1)}, bf16[2,256,256]{2,1,0:T(8,128)(2,1)}, u32[]{:S(2)}) copy-start(bf16[2,256,256]{2,1,0:T(8,128)(2,1)} %constant.5.clone.low) | copy-start | bytes 786436
  4.7 0.9 %copy-start.4 = (bf16[2,256,256]{2,1,0:T(8,128)(2,1)S(1)}, bf16[2,256,256]{2,1,0:T(8,128)(2,1)}, u32[]{:S(2)}) copy-start(bf16[2,256,256]{2,1,0:T(8,128)(2,1)} %constant.4.clone.high) | copy-start | bytes 786436

commit v2 on v1

--- a/solution.py
+++ b/solution.py
@@ -22,10 +22,10 @@
     chirp = np.exp(0.5j * frequency.astype(np.float64) ** 2 / side)
     column = np.fft.ifft(chirp)
     matrix = column[(counter[:, None] - counter[None, :]) % side]
-    parts = np.stack([matrix.real, matrix.imag])
+    parts = np.concatenate([matrix.real, matrix.imag], axis=1)
     high = parts.astype(ml_dtypes.bfloat16)
     low = (parts - high.astype(np.float64)).astype(ml_dtypes.bfloat16)
-    return high, low
+    return np.stack([high, low])
 
 
 def dot(a, b):
@@ -55,22 +55,25 @@
 def kernel(
     depth_count,
     probe_count,
+    waves_hbm,
+    layers_hbm,
+    residual_hbm,
+    offsets,
+    slot,
+    table_hbm,
+    out,
     waves,
     layers,
     residual,
-    offsets,
-    slot,
-    high,
-    low,
-    out,
+    table,
     hand_out,
     hand_in,
-    turned_high,
-    turned_low,
+    turned,
     grads,
     corners,
     strips_out,
     strips_in,
+    load_sems,
     hand_sems,
     grad_sems,
     corner_sems,
@@ -96,6 +99,27 @@
     def _():
         pl.semaphore_signal(barrier, inc=1, device_id={"depth": depth + 1}, device_id_type=MESH)
 
+    load_residual = pltpu.make_async_copy(residual_hbm, residual, load_sems.at[0])
+    load_layers = pltpu.make_async_copy(layers_hbm, layers, load_sems.at[1])
+    load_waves = pltpu.make_async_copy(waves_hbm, waves, load_sems.at[2])
+    load_table = pltpu.make_async_copy(table_hbm, table, load_sems.at[3])
+
+    @pl.when(is_top)
+    def _():
+        load_residual.start()
+
+    if depth_count > 1:
+
+        @pl.when(has_below)
+        def _():
+            load_layers.start()
+
+        @pl.when(jnp.logical_not(is_top))
+        def _():
+            load_table.start()
+
+    load_waves.start()
+
     own_slot = slot[0]
     top_row = offsets[own_slot, 0]
     left_column = offsets[own_slot, 1]
@@ -162,46 +186,54 @@
 
     @pl.when(is_top)
     def _():
+        load_residual.wait()
         if depth_count > 1:
+            load_layers.wait()
             for part in range(CHUNKS):
                 window = pl.ds(part * step, step)
                 hand_down(part, residual[0, 0, window, :], residual[0, 1, window, :])
+        load_waves.wait()
         for part in range(CHUNKS):
             window = pl.ds(part * step, step)
             give_gradient(part, residual[0, 0, window, :], residual[0, 1, window, :])
 
     if depth_count > 1:
 
-        @pl.when(depth < depth_count - 1)
+        @pl.when(jnp.logical_not(is_top))
         def _():
+            load_table.wait()
+            load_waves.wait()
+            if depth_count > 2:
+
+                @pl.when(has_below)
+                def _():
+                    load_layers.wait()
+
             for part in range(CHUNKS):
                 window = pl.ds(part * step, step)
                 hand_copy(part).wait_recv()
-                real, imag = hand_in[0, window, :], hand_in[1, window, :]
-
-                def times(index):
-                    return (
-                        dot(real, high[index]) + dot(real, low[index]),
-                        dot(imag, high[index]) + dot(imag, low[index]),
-                    )
-
-                real_cos, imag_cos = times(0)
-                real_sin, imag_sin = times(1)
-                for index, value in enumerate((real_cos - imag_sin, real_sin + imag_cos)):
-                    turned_high[index, window, :], turned_low[index, window, :] = split(value)
+                real = dot(hand_in[0, window, :], table[0]) + dot(hand_in[0, window, :], table[1])
+                imag = dot(hand_in[1, window, :], table[0]) + dot(hand_in[1, window, :], table[1])
+                product = real[:, :side] - imag[:, side:], real[:, side:] + imag[:, :side]
+                for c in range(2):
+                    top, rest = split(product[c])
+                    turned[0, window, pl.ds(c * side, side)] = top
+                    turned[1, window, pl.ds(c * side, side)] = rest
 
             for part in range(CHUNKS):
                 window = pl.ds(part * step, step)
 
-                def from_left(table, field):
+                def from_left(index):
+                    columns = pl.ds(index * side, side)
                     return (
-                        dot(high[table, window, :], turned_high[field])
-                        + dot(low[table, window, :], turned_high[field])
-                        + dot(high[table, window, :], turned_low[field])
+                        dot(table[0, window, columns], turned[0])
+                        + dot(table[1, window, columns], turned[0])
+                        + dot(table[0, window, columns], turned[1])
                     )
 
-                real = from_left(0, 0) - from_left(1, 1)
-                imag = from_left(0, 1) + from_left(1, 0)
+                by_real, by_imag = from_left(0), from_left(1)
+                real = by_real[:, :side] - by_imag[:, side:]
+                imag = by_real[:, side:] + by_imag[:, :side]
                 if depth_count > 2:
 
                     @pl.when(has_below)
@@ -274,24 +306,29 @@
 
 def per_device(depth_count, probe_count, tile_count, waves, layers, residual, offsets, slot):
     side = waves.shape[-1]
-    high, low = propagator(side)
+    table = propagator(side)
     rows, columns = OBJ // probe_count, OBJ // tile_count
     vmem = pl.BlockSpec(memory_space=pltpu.VMEM)
     smem = pl.BlockSpec(memory_space=pltpu.SMEM)
+    hbm = pl.BlockSpec(memory_space=pltpu.HBM)
     return pl.pallas_call(
         functools.partial(kernel, depth_count, probe_count),
         out_shape=jax.ShapeDtypeStruct((2, 1, rows, columns), F32),
-        in_specs=[vmem, vmem, vmem, smem, smem, vmem, vmem],
+        in_specs=[hbm, hbm, hbm, smem, smem, hbm],
         out_specs=vmem,
         scratch_shapes=[
+            pltpu.VMEM(waves.shape, waves.dtype),
+            pltpu.VMEM(layers.shape, layers.dtype),
+            pltpu.VMEM(residual.shape, residual.dtype),
+            pltpu.VMEM(table.shape, BF16),
             pltpu.VMEM((2, side, side), BF16),
             pltpu.VMEM((2, side, side), BF16),
-            pltpu.VMEM((2, side, side), BF16),
-            pltpu.VMEM((2, side, side), BF16),
+            pltpu.VMEM((2, side, 2 * side), BF16),
             pltpu.VMEM((2, 2, side, side), BF16),
             pltpu.VMEM((2, 16, side), jnp.int32),
             pltpu.VMEM((probe_count - 1, 2, rows, columns), BF16),
             pltpu.VMEM((probe_count - 1, 2, rows, columns), BF16),
+            pltpu.SemaphoreType.DMA((4,)),
             pltpu.SemaphoreType.DMA((2, CHUNKS)),
             pltpu.SemaphoreType.DMA((2, CHUNKS)),
             pltpu.SemaphoreType.DMA((2,)),
@@ -300,7 +337,7 @@
         compiler_params=pltpu.CompilerParams(
             collective_id=0, has_side_effects=True, vmem_limit_bytes=32 * 1024 * 1024
         ),
-    )(waves, layers, residual, offsets, slot, jnp.asarray(high), jnp.asarray(low))
+    )(waves, layers, residual, offsets, slot, jnp.asarray(table))
 
 
 def solution(mesh):

time: 35.7 us -> 34.7 us (0.972)
  local copies, waits for them, and re-layouts: 5.64 us -> 4.78 us
    unnamed x14 -> x12, local copies, waits for them, and re-layouts: 5.64 us -> 4.78 us
where the time goes in v2:
time: 34.7 us; the launch traced here: 34.5 us
  Pallas kernels  29 us (84%)
  local copies, waits for them, and re-layouts  4.78 us (14%)
  between operations  0.68 us (2%)
    pallas_call x1, Pallas kernels, per_device(): pl.pallas_call(functools.partial(kernel, depth_count, probe_count), out_s...  29 us
    unnamed x12, local copies, waits for them, and re-layouts  4.78 us

profile of v2, /device:TPU:0, one launch (start us, length us, event | category | flops | bytes accessed | tf_op | source)
XLA Modules:
  0.0 34.5 jit_solution(8254574818368946717)
XLA Ops:
  0.0 0.0 copy-start.4
  0.7 0.0 copy-done.4
  0.7 0.1 copy.7.offsets
  0.8 0.0 copy-start
  0.8 1.0 %copy-done = f32[1,2,256,256]{3,2,1,0:T(8,128)S(1)} copy-done((f32[1,2,256,256]{3,2,1,0:T(8,128)S(1)}, f32[1,2,256,256]{3,2,1,0:T(8,128)}, u32[]{:S(2)}) %copy-start) | copy-done | bytes 524312
  1.8 0.0 copy-start.1
  1.8 1.0 %copy-done.1 = bf16[2,256,512]{2,1,0:T(8,128)(2,1)S(1)} copy-done((bf16[2,256,512]{2,1,0:T(8,128)(2,1)S(1)}, bf16[2,256,512]{2,1,0:T(8,128)(2,1)}, u32[]{:S(2)}) %copy-start.1) | copy-done | bytes 524312
  2.8 0.0 copy-start.2
  2.8 0.9 %copy-done.2 = bf16[1,1,2,256,256]{4,3,2,1,0:T(8,128)(2,1)S(1)} copy-done((bf16[1,1,2,256,256]{4,3,2,1,0:T(8,128)(2,1)S(1)}, bf16[1,1,2,256,256]{4,3,2,1,0:T(8,128)(2,1)}, u32[]{:S(2)}) %copy-start.2) | copy-done | bytes 262168
  3.8 0.0 copy-start.3
  3.8 0.9 %copy-done.3 = bf16[1,1,2,256,256]{4,3,2,1,0:T(8,128)(2,1)S(1)} copy-done((bf16[1,1,2,256,256]{4,3,2,1,0:T(8,128)(2,1)S(1)}, bf16[1,1,2,256,256]{4,3,2,1,0:T(8,128)(2,1)}, u32[]{:S(2)}) %copy-start.3) | copy-done | bytes 262168
  4.7 29.0 %shard_map.64 = f32[2,1,128,256]{3,2,1,0:T(8,128)S(1)} custom-call(bf16[1,1,2,256,256]{4,3,2,1,0:T(8,128)(2,1)S(1)} %copy-done.2, bf16[1,1,2,256,256]{4,3,2,1,0:T(8,128)(2,1)S(1)} %copy-done.3, f32[1,2,256,256]{3,2,1,0:T(8,128)S(1)} %copy-done, s32[8,2]{1,0:T(8,128)S(1)} %copy.7.offsets, s32[1]{0:T(128)S(6)} %copy.9.slot, bf16[2,256,512]{2,1,0:T(8,128)(2,1)S(1)} %copy-done.1), custom_call_target="tpu_custom_call" | custom-call | tf_op jit(solution)/shard_map/pallas_call | solution.py:314
  33.7 0.7 %copy.10 = f32[2,1,128,256]{3,2,1,0:T(8,128)} copy(f32[2,1,128,256]{3,2,1,0:T(8,128)S(1)} %shard_map.64) | data formatting | bytes 524288
Async XLA Ops:
  0.0 0.7 %copy-start.4 = (s32[8,2]{0,1:T(2,128)S(1)}, s32[8,2]{0,1:T(2,128)}, u32[]{:S(2)}) copy-start(s32[8,2]{0,1:T(2,128)} %param.9) | copy-start | bytes 196
  0.8 1.0 %copy-start = (f32[1,2,256,256]{3,2,1,0:T(8,128)S(1)}, f32[1,2,256,256]{3,2,1,0:T(8,128)}, u32[]{:S(2)}) copy-start(f32[1,2,256,256]{3,2,1,0:T(8,128)} %residual_hbm.1) | copy-start | bytes 1572868
  1.8 1.0 %copy-start.1 = (bf16[2,256,512]{2,1,0:T(8,128)(2,1)S(1)}, bf16[2,256,512]{2,1,0:T(8,128)(2,1)}, u32[]{:S(2)}) copy-start(bf16[2,256,512]{2,1,0:T(8,128)(2,1)} %constant.2.clone.table_hbm) | copy-start | bytes 1572868
  2.8 0.9 %copy-start.2 = (bf16[1,1,2,256,256]{4,3,2,1,0:T(8,128)(2,1)S(1)}, bf16[1,1,2,256,256]{4,3,2,1,0:T(8,128)(2,1)}, u32[]{:S(2)}) copy-start(bf16[1,1,2,256,256]{4,3,2,1,0:T(8,128)(2,1)} %waves_hbm.1) | copy-start | bytes 786436
  3.8 0.9 %copy-start.3 = (bf16[1,1,2,256,256]{4,3,2,1,0:T(8,128)(2,1)S(1)}, bf16[1,1,2,256,256]{4,3,2,1,0:T(8,128)(2,1)}, u32[]{:S(2)}) copy-start(bf16[1,1,2,256,256]{4,3,2,1,0:T(8,128)(2,1)} %layers_hbm.1) | copy-start | bytes 786436

commit v3 on v2

--- a/solution.py
+++ b/solution.py
@@ -335,7 +335,7 @@
             pltpu.SemaphoreType.DMA((2, probe_count - 1)),
         ],
         compiler_params=pltpu.CompilerParams(
-            collective_id=0, has_side_effects=True, vmem_limit_bytes=32 * 1024 * 1024
+            collective_id=0, has_side_effects=True, vmem_limit_bytes=60 * 1024 * 1024
         ),
     )(waves, layers, residual, offsets, slot, jnp.asarray(table))
 

time: 34.7 us -> 33 us (0.951)
  local copies, waits for them, and re-layouts: 4.78 us -> 2.35 us
  Pallas kernels: 29 us -> 29.8 us
    unnamed x12 -> x4, local copies, waits for them, and re-layouts: 4.78 us -> 2.35 us
    pallas_call x1, Pallas kernels: 29 us -> 29.8 us  [per_device(): pl.pallas_call(functools.partial(kernel, depth_count, probe_count), out_s...]
where the time goes in v3:
time: 33 us; the launch traced here: 32.8 us
  Pallas kernels  29.8 us (90%)
  local copies, waits for them, and re-layouts  2.35 us (7%)
  between operations  0.68 us (2%)
    pallas_call x1, Pallas kernels, per_device(): pl.pallas_call(functools.partial(kernel, depth_count, probe_count), out_s...  29.8 us
    unnamed x4, local copies, waits for them, and re-layouts  2.35 us

profile of v3, /device:TPU:0, one launch (start us, length us, event | category | flops | bytes accessed | tf_op | source)
XLA Modules:
  0.0 32.8 jit_solution(2385599929273193455)
XLA Ops:
  0.0 0.0 copy-start
  0.7 0.0 copy-done
  0.7 0.7 %copy.7.offsets = s32[8,2]{1,0:T(8,128)} copy(s32[8,2]{0,1:T(2,128)S(1)} %copy-done) | data formatting | bytes 128 | tf_op args[3]
  1.4 29.8 %shard_map.64 = f32[2,1,128,256]{3,2,1,0:T(8,128)} custom-call(bf16[1,1,2,256,256]{4,3,2,1,0:T(8,128)(2,1)} %waves_hbm.1, bf16[1,1,2,256,256]{4,3,2,1,0:T(8,128)(2,1)} %layers_hbm.1, f32[1,2,256,256]{3,2,1,0:T(8,128)} %residual_hbm.1, s32[8,2]{1,0:T(8,128)} %copy.7.offsets, s32[1]{0:T(128)S(6)} %copy.9.slot, bf16[2,256,512]{2,1,0:T(8,128)(2,1)} %constant.2.clone.table_hbm), custom_call_target="tpu_custom_call" | custom-call | tf_op jit(solution)/shard_map/pallas_call | solution.py:314
  31.2 1.7 %copy.10 = f32[2,1,128,256]{3,2,1,0:T(8,128)} copy(f32[2,1,128,256]{3,2,1,0:T(8,128)} %shard_map.64) | data formatting | bytes 524288
Async XLA Ops:
  0.0 0.7 %copy-start = (s32[8,2]{0,1:T(2,128)S(1)}, s32[8,2]{0,1:T(2,128)}, u32[]{:S(2)}) copy-start(s32[8,2]{0,1:T(2,128)} %param.9) | copy-start | bytes 196

commit v4 on v3

--- a/solution.py
+++ b/solution.py
@@ -71,12 +71,15 @@
     turned,
     grads,
     corners,
+    pair_out,
+    pair_in,
     strips_out,
     strips_in,
     load_sems,
     hand_sems,
     grad_sems,
     corner_sems,
+    pair_sems,
     strip_sems,
 ):
     side = waves.shape[-1]
@@ -85,11 +88,12 @@
     depth = lax.axis_index("depth")
     probe = lax.axis_index("probe")
     tile = lax.axis_index("tile")
+    partner = flip(probe, 1, probe_count)
     is_top = depth == depth_count - 1
     has_below = depth > 0
 
     barrier = pltpu.get_barrier_semaphore()
-    for mask in range(1, probe_count):
+    for mask in [1, *range(2, probe_count, 2)]:
         pl.semaphore_signal(
             barrier, inc=1, device_id={"probe": flip(probe, mask, probe_count)}, device_id_type=MESH
         )
@@ -121,18 +125,18 @@
     load_waves.start()
 
     own_slot = slot[0]
-    top_row = offsets[own_slot, 0]
-    left_column = offsets[own_slot, 1]
+    top_row = offsets[0, own_slot]
+    left_column = offsets[1, own_slot]
     corners[0, 0:8, :] = jnp.full((8, side), top_row, jnp.int32)
     corners[0, 8:16, :] = jnp.full((8, side), left_column, jnp.int32)
 
     @pl.when(has_below)
     def _():
-        pl.semaphore_wait(barrier, probe_count + 1)
+        pl.semaphore_wait(barrier, probe_count // 2 + 2)
 
     @pl.when(jnp.logical_not(has_below))
     def _():
-        pl.semaphore_wait(barrier, probe_count)
+        pl.semaphore_wait(barrier, probe_count // 2 + 1)
 
     corner_copy = pltpu.make_async_remote_copy(
         src_ref=corners.at[0],
@@ -269,34 +273,55 @@
         peer_rows = onehot(shifted == peer_row)
         return [dot(own_rows, placed[c][0]) + dot(peer_rows, placed[c][1]) for c in range(2)]
 
-    def strip_copy(mask):
+    def pair_copy(mask, c):
         return pltpu.make_async_remote_copy(
-            src_ref=strips_out.at[mask - 1],
-            dst_ref=strips_in.at[mask - 1],
-            send_sem=strip_sems.at[0, mask - 1],
-            recv_sem=strip_sems.at[1, mask - 1],
+            src_ref=pair_out.at[mask // 2, c],
+            dst_ref=pair_in.at[mask // 2, c],
+            send_sem=pair_sems.at[0, mask // 2, c],
+            recv_sem=pair_sems.at[1, mask // 2, c],
+            device_id={"probe": partner},
+            device_id_type=MESH,
+        )
+
+    def strip_copy(mask, c):
+        return pltpu.make_async_remote_copy(
+            src_ref=strips_out.at[mask // 2 - 1, c],
+            dst_ref=strips_in.at[mask // 2 - 1, c],
+            send_sem=strip_sems.at[0, mask // 2 - 1, c],
+            recv_sem=strip_sems.at[1, mask // 2 - 1, c],
             device_id={"probe": flip(probe, mask, probe_count)},
             device_id_type=MESH,
         )
 
-    for mask in range(probe_count - 1, 0, -1):
-        real, imag = strip(flip(probe, mask, probe_count))
-        strips_out[mask - 1, 0] = real.astype(BF16)
-        strips_out[mask - 1, 1] = imag.astype(BF16)
-        strip_copy(mask).start()
+    for mask in range(probe_count - 2, -1, -2):
+        value = strip(flip(partner, mask, probe_count))
+        for c in range(2):
+            pair_out[mask // 2, c] = value[c].astype(BF16)
+            pair_copy(mask, c).start()
+    for mask in range(probe_count - 2, 0, -2):
+        value = strip(flip(probe, mask, probe_count))
+        for c in range(2):
+            pair_copy(mask, c).wait_recv()
+            strips_out[mask // 2 - 1, c] = (value[c] + pair_in[mask // 2, c].astype(F32)).astype(BF16)
+            strip_copy(mask, c).start()
     total = strip(probe)
     for c in range(2):
-        out[c, 0] = total[c]
-    for mask in range(1, probe_count):
-        strip_copy(mask).wait_recv()
-        for c in range(2):
-            out[c, 0] += strips_in[mask - 1, c].astype(F32)
+        pair_copy(0, c).wait_recv()
+        out[c, 0] = total[c] + pair_in[0, c].astype(F32)
+    for mask in range(probe_count - 2, 0, -2):
+        for c in range(2):
+            strip_copy(mask, c).wait_recv()
+            out[c, 0] += strips_in[mask // 2 - 1, c].astype(F32)
 
     corner_copy.wait_send()
     for part in range(CHUNKS):
         grad_copy(part).wait_send()
-    for mask in range(1, probe_count):
-        strip_copy(mask).wait_send()
+    for mask in range(0, probe_count, 2):
+        for c in range(2):
+            pair_copy(mask, c).wait_send()
+    for mask in range(2, probe_count, 2):
+        for c in range(2):
+            strip_copy(mask, c).wait_send()
 
     @pl.when(has_below)
     def _():
@@ -326,18 +351,21 @@
             pltpu.VMEM((2, side, 2 * side), BF16),
             pltpu.VMEM((2, 2, side, side), BF16),
             pltpu.VMEM((2, 16, side), jnp.int32),
-            pltpu.VMEM((probe_count - 1, 2, rows, columns), BF16),
-            pltpu.VMEM((probe_count - 1, 2, rows, columns), BF16),
+            pltpu.VMEM((probe_count // 2, 2, rows, columns), BF16),
+            pltpu.VMEM((probe_count // 2, 2, rows, columns), BF16),
+            pltpu.VMEM((probe_count // 2 - 1, 2, rows, columns), BF16),
+            pltpu.VMEM((probe_count // 2 - 1, 2, rows, columns), BF16),
             pltpu.SemaphoreType.DMA((4,)),
             pltpu.SemaphoreType.DMA((2, CHUNKS)),
             pltpu.SemaphoreType.DMA((2, CHUNKS)),
             pltpu.SemaphoreType.DMA((2,)),
-            pltpu.SemaphoreType.DMA((2, probe_count - 1)),
+            pltpu.SemaphoreType.DMA((2, probe_count // 2, 2)),
+            pltpu.SemaphoreType.DMA((2, probe_count // 2 - 1, 2)),
         ],
         compiler_params=pltpu.CompilerParams(
             collective_id=0, has_side_effects=True, vmem_limit_bytes=60 * 1024 * 1024
         ),
-    )(waves, layers, residual, offsets, slot, jnp.asarray(table))
+    )(waves, layers, residual, offsets.T, slot, jnp.asarray(table))
 
 
 def solution(mesh):

time: 33 us -> 31.1 us (0.942)
  Pallas kernels: 29.8 us -> 28.6 us
  local copies, waits for them, and re-layouts: 2.35 us -> 1.67 us
    pallas_call x1, Pallas kernels: 29.8 us -> 28.6 us  [per_device(): pl.pallas_call(functools.partial(kernel, depth_count, probe_count), out_s...]
    unnamed x4 -> x1, local copies, waits for them, and re-layouts: 2.35 us -> 1.67 us
where the time goes in v4:
time: 31.1 us; the launch traced here: 31 us
  Pallas kernels  28.6 us (92%)
  local copies, waits for them, and re-layouts  1.67 us (5%)
  between operations  0.66 us (2%)
    pallas_call x1, Pallas kernels, per_device(): pl.pallas_call(functools.partial(kernel, depth_count, probe_count), out_s...  28.6 us
    unnamed x1, local copies, waits for them, and re-layouts  1.67 us

profile of v4, /device:TPU:0, one launch (start us, length us, event | category | flops | bytes accessed | tf_op | source)
XLA Modules:
  0.0 31.0 jit_solution(564336575413074847)
XLA Ops:
  0.7 28.6 %shard_map.64 = f32[2,1,128,256]{3,2,1,0:T(8,128)} custom-call(bf16[1,1,2,256,256]{4,3,2,1,0:T(8,128)(2,1)} %waves_hbm.1, bf16[1,1,2,256,256]{4,3,2,1,0:T(8,128)(2,1)} %layers_hbm.1, f32[1,2,256,256]{3,2,1,0:T(8,128)} %residual_hbm.1, s32[2,8]{1,0:T(2,128)} %bitcast.1, s32[1]{0:T(128)S(6)} %copy.8.slot, bf16[2,256,512]{2,1,0:T(8,128)(2,1)} %constant.2.clone.table_hbm), custom_call_target="tpu_custom_call" | custom-call | tf_op jit(solution)/shard_map/pallas_call | solution.py:339
  29.3 1.7 %copy.9 = f32[2,1,128,256]{3,2,1,0:T(8,128)} copy(f32[2,1,128,256]{3,2,1,0:T(8,128)} %shard_map.64) | data formatting | bytes 524288

commit v5 on v2

--- a/solution.py
+++ b/solution.py
@@ -10,7 +10,7 @@
 from jax.sharding import PartitionSpec as P
 
 OBJ = 512
-CHUNKS = 4
+CHUNKS = 2
 MESH = pl.DeviceIdType.MESH
 F32 = jnp.float32
 BF16 = jnp.bfloat16
@@ -71,13 +71,20 @@
     turned,
     grads,
     corners,
-    strips_out,
-    strips_in,
+    direct_out,
+    direct_in,
+    pair_out,
+    pair_in,
+    sum_out,
+    sum_in,
+    held,
     load_sems,
     hand_sems,
     grad_sems,
     corner_sems,
-    strip_sems,
+    direct_sems,
+    pair_sems,
+    sum_sems,
 ):
     side = waves.shape[-1]
     rows, columns = out.shape[2], out.shape[3]
@@ -121,8 +128,8 @@
     load_waves.start()
 
     own_slot = slot[0]
-    top_row = offsets[own_slot, 0]
-    left_column = offsets[own_slot, 1]
+    top_row = offsets[0, own_slot]
+    left_column = offsets[1, own_slot]
     corners[0, 0:8, :] = jnp.full((8, side), top_row, jnp.int32)
     corners[0, 8:16, :] = jnp.full((8, side), left_column, jnp.int32)
 
@@ -269,34 +276,81 @@
         peer_rows = onehot(shifted == peer_row)
         return [dot(own_rows, placed[c][0]) + dot(peer_rows, placed[c][1]) for c in range(2)]
 
-    def strip_copy(mask):
+    def direct_copy(mask, c):
+        place = mask - 1 if c == 0 else probe_count - 1
         return pltpu.make_async_remote_copy(
-            src_ref=strips_out.at[mask - 1],
-            dst_ref=strips_in.at[mask - 1],
-            send_sem=strip_sems.at[0, mask - 1],
-            recv_sem=strip_sems.at[1, mask - 1],
+            src_ref=direct_out.at[place],
+            dst_ref=direct_in.at[place],
+            send_sem=direct_sems.at[0, place],
+            recv_sem=direct_sems.at[1, place],
             device_id={"probe": flip(probe, mask, probe_count)},
             device_id_type=MESH,
         )
 
-    for mask in range(probe_count - 1, 0, -1):
+    def pair_copy(place):
+        return pltpu.make_async_remote_copy(
+            src_ref=pair_out.at[place],
+            dst_ref=pair_in.at[place],
+            send_sem=pair_sems.at[0, place],
+            recv_sem=pair_sems.at[1, place],
+            device_id={"probe": flip(probe, 1, probe_count)},
+            device_id_type=MESH,
+        )
+
+    def sum_copy(place):
+        return pltpu.make_async_remote_copy(
+            src_ref=sum_out.at[place],
+            dst_ref=sum_in.at[place],
+            send_sem=sum_sems.at[0, place],
+            recv_sem=sum_sems.at[1, place],
+            device_id={"probe": flip(probe, 2 * place + 2, probe_count)},
+            device_id_type=MESH,
+        )
+
+    others = range(probe_count // 2 - 1, 0, -1)
+    for other in others:
+        mask = 2 * other + 1
         real, imag = strip(flip(probe, mask, probe_count))
-        strips_out[mask - 1, 0] = real.astype(BF16)
-        strips_out[mask - 1, 1] = imag.astype(BF16)
-        strip_copy(mask).start()
+        pair_out[other - 1] = imag.astype(BF16)
+        pair_copy(other - 1).start()
+        direct_out[mask - 1] = real.astype(BF16)
+        direct_copy(mask, 0).start()
+    for other in others:
+        mask = 2 * other
+        real, imag = strip(flip(probe, mask, probe_count))
+        direct_out[mask - 1] = real.astype(BF16)
+        direct_copy(mask, 0).start()
+        held[other - 1] = imag
+    real, imag = strip(flip(probe, 1, probe_count))
+    direct_out[0] = real.astype(BF16)
+    direct_out[probe_count - 1] = imag.astype(BF16)
+    for other in others:
+        pair_copy(other - 1).wait_recv()
+        sum_out[other - 1] = (held[other - 1] + pair_in[other - 1].astype(F32)).astype(BF16)
+        sum_copy(other - 1).start()
+    direct_copy(1, 0).start()
+    direct_copy(1, 1).start()
     total = strip(probe)
     for c in range(2):
         out[c, 0] = total[c]
-    for mask in range(1, probe_count):
-        strip_copy(mask).wait_recv()
-        for c in range(2):
-            out[c, 0] += strips_in[mask - 1, c].astype(F32)
+    for mask in range(probe_count - 1, 0, -1):
+        direct_copy(mask, 0).wait_recv()
+        out[0, 0] += direct_in[mask - 1].astype(F32)
+    direct_copy(1, 1).wait_recv()
+    out[1, 0] += direct_in[probe_count - 1].astype(F32)
+    for other in others:
+        sum_copy(other - 1).wait_recv()
+        out[1, 0] += sum_in[other - 1].astype(F32)
 
     corner_copy.wait_send()
     for part in range(CHUNKS):
         grad_copy(part).wait_send()
     for mask in range(1, probe_count):
-        strip_copy(mask).wait_send()
+        direct_copy(mask, 0).wait_send()
+    direct_copy(1, 1).wait_send()
+    for other in others:
+        pair_copy(other - 1).wait_send()
+        sum_copy(other - 1).wait_send()
 
     @pl.when(has_below)
     def _():
@@ -308,6 +362,7 @@
     side = waves.shape[-1]
     table = propagator(side)
     rows, columns = OBJ // probe_count, OBJ // tile_count
+    others = probe_count // 2 - 1
     vmem = pl.BlockSpec(memory_space=pltpu.VMEM)
     smem = pl.BlockSpec(memory_space=pltpu.SMEM)
     hbm = pl.BlockSpec(memory_space=pltpu.HBM)
@@ -326,18 +381,30 @@
             pltpu.VMEM((2, side, 2 * side), BF16),
             pltpu.VMEM((2, 2, side, side), BF16),
             pltpu.VMEM((2, 16, side), jnp.int32),
-            pltpu.VMEM((probe_count - 1, 2, rows, columns), BF16),
-            pltpu.VMEM((probe_count - 1, 2, rows, columns), BF16),
+            pltpu.VMEM((probe_count, rows, columns), BF16),
+            pltpu.VMEM((probe_count, rows, columns), BF16),
+            pltpu.VMEM((others, rows, columns), BF16),
+            pltpu.VMEM((others, rows, columns), BF16),
+            pltpu.VMEM((others, rows, columns), BF16),
+            pltpu.VMEM((others, rows, columns), BF16),
+            pltpu.VMEM((others, rows, columns), F32),
             pltpu.SemaphoreType.DMA((4,)),
             pltpu.SemaphoreType.DMA((2, CHUNKS)),
             pltpu.SemaphoreType.DMA((2, CHUNKS)),
             pltpu.SemaphoreType.DMA((2,)),
-            pltpu.SemaphoreType.DMA((2, probe_count - 1)),
+            pltpu.SemaphoreType.DMA((2, probe_count)),
+            pltpu.SemaphoreType.DMA((2, others)),
+            pltpu.SemaphoreType.DMA((2, others)),
         ],
         compiler_params=pltpu.CompilerParams(
             collective_id=0, has_side_effects=True, vmem_limit_bytes=32 * 1024 * 1024
         ),
-    )(waves, layers, residual, offsets, slot, jnp.asarray(table))
+    )(
+        *(pltpu.with_memory_space_constraint(x, pltpu.HBM) for x in (waves, layers, residual)),
+        offsets.T,
+        slot,
+        pltpu.with_memory_space_constraint(jnp.asarray(table), pltpu.HBM),
+    )
 
 
 def solution(mesh):

time: 34.7 us -> 28.1 us (0.81)
  local copies, waits for them, and re-layouts: 4.78 us -> 1.38 us
  Pallas kernels: 29 us -> 25.9 us
    unnamed x12 -> x3, local copies, waits for them, and re-layouts: 4.78 us -> 1.38 us
    pallas_call x1, Pallas kernels: 29 us -> 25.9 us  [per_device(): pl.pallas_call(functools.partial(kernel, depth_count, probe_count), out_s...]
where the time goes in v5:
time: 28.1 us; the launch traced here: 28 us
  Pallas kernels  25.9 us (92%)
  local copies, waits for them, and re-layouts  1.38 us (5%)
  between operations  0.67 us (2%)
    pallas_call x1, Pallas kernels, per_device(): pl.pallas_call(functools.partial(kernel, depth_count, probe_count), out_s...  25.9 us
    unnamed x3, local copies, waits for them, and re-layouts  1.38 us

profile of v5, /device:TPU:0, one launch (start us, length us, event | category | flops | bytes accessed | tf_op | source)
XLA Modules:
  0.0 28.0 jit_solution(2154045327119778579)
XLA Ops:
  0.7 0.0 copy-start
  0.7 0.7 %copy-done = s32[8,2]{0,1:T(2,128)S(1)} copy-done((s32[8,2]{0,1:T(2,128)S(1)}, s32[8,2]{0,1:T(2,128)}, u32[]{:S(2)}) %copy-start) | copy-done | bytes 88
  1.3 25.9 %shard_map.64 = f32[2,1,128,256]{3,2,1,0:T(8,128)S(1)} custom-call(bf16[1,1,2,256,256]{4,3,2,1,0:T(8,128)(2,1)} %waves_hbm.1, bf16[1,1,2,256,256]{4,3,2,1,0:T(8,128)(2,1)} %layers_hbm.1, f32[1,2,256,256]{3,2,1,0:T(8,128)} %residual_hbm.1, s32[2,8]{1,0:T(2,128)S(1)} %bitcast.1, s32[1]{0:T(128)S(6)} %copy.8.slot, bf16[2,256,512]{2,1,0:T(8,128)(2,1)} %constant.2.clone.table_hbm), custom_call_target="tpu_custom_call" | custom-call | tf_op jit(solution)/shard_map/pallas_call | solution.py:369
  27.3 0.7 %copy.9 = f32[2,1,128,256]{3,2,1,0:T(8,128)} copy(f32[2,1,128,256]{3,2,1,0:T(8,128)S(1)} %shard_map.64) | data formatting | bytes 524288
Async XLA Ops:
  0.7 0.7 %copy-start = (s32[8,2]{0,1:T(2,128)S(1)}, s32[8,2]{0,1:T(2,128)}, u32[]{:S(2)}) copy-start(s32[8,2]{0,1:T(2,128)} %param.9) | copy-start | bytes 196

commit v6 on v5

--- a/solution.py
+++ b/solution.py
@@ -10,7 +10,7 @@
 from jax.sharding import PartitionSpec as P
 
 OBJ = 512
-CHUNKS = 2
+CHUNKS = 1
 MESH = pl.DeviceIdType.MESH
 F32 = jnp.float32
 BF16 = jnp.bfloat16
@@ -223,9 +223,7 @@
                 imag = dot(hand_in[1, window, :], table[0]) + dot(hand_in[1, window, :], table[1])
                 product = real[:, :side] - imag[:, side:], real[:, side:] + imag[:, :side]
                 for c in range(2):
-                    top, rest = split(product[c])
-                    turned[0, window, pl.ds(c * side, side)] = top
-                    turned[1, window, pl.ds(c * side, side)] = rest
+                    turned[window, pl.ds(c * side, side)] = product[c].astype(BF16)
 
             for part in range(CHUNKS):
                 window = pl.ds(part * step, step)
@@ -233,9 +231,7 @@
                 def from_left(index):
                     columns = pl.ds(index * side, side)
                     return (
-                        dot(table[0, window, columns], turned[0])
-                        + dot(table[1, window, columns], turned[0])
-                        + dot(table[0, window, columns], turned[1])
+                        dot(table[0, window, columns], turned[...]) + dot(table[1, window, columns], turned[...])
                     )
 
                 by_real, by_imag = from_left(0), from_left(1)
@@ -324,12 +320,12 @@
     real, imag = strip(flip(probe, 1, probe_count))
     direct_out[0] = real.astype(BF16)
     direct_out[probe_count - 1] = imag.astype(BF16)
+    direct_copy(1, 0).start()
+    direct_copy(1, 1).start()
     for other in others:
         pair_copy(other - 1).wait_recv()
         sum_out[other - 1] = (held[other - 1] + pair_in[other - 1].astype(F32)).astype(BF16)
         sum_copy(other - 1).start()
-    direct_copy(1, 0).start()
-    direct_copy(1, 1).start()
     total = strip(probe)
     for c in range(2):
         out[c, 0] = total[c]
@@ -378,7 +374,7 @@
             pltpu.VMEM(table.shape, BF16),
             pltpu.VMEM((2, side, side), BF16),
             pltpu.VMEM((2, side, side), BF16),
-            pltpu.VMEM((2, side, 2 * side), BF16),
+            pltpu.VMEM((side, 2 * side), BF16),
             pltpu.VMEM((2, 2, side, side), BF16),
             pltpu.VMEM((2, 16, side), jnp.int32),
             pltpu.VMEM((probe_count, rows, columns), BF16),

time: 28.1 us -> 27.2 us (0.968)
  Pallas kernels: 25.9 us -> 25 us
    pallas_call x1, Pallas kernels: 25.9 us -> 25 us  [per_device(): pl.pallas_call(functools.partial(kernel, depth_count, probe_count), out_s...]
where the time goes in v6:
time: 27.2 us; the launch traced here: 27.1 us
  Pallas kernels  25 us (92%)
  local copies, waits for them, and re-layouts  1.38 us (5%)
  between operations  0.67 us (2%)
    pallas_call x1, Pallas kernels, per_device(): pl.pallas_call(functools.partial(kernel, depth_count, probe_count), out_s...  25 us
    unnamed x3, local copies, waits for them, and re-layouts  1.38 us

profile of v6, /device:TPU:0, one launch (start us, length us, event | category | flops | bytes accessed | tf_op | source)
XLA Modules:
  0.0 27.1 jit_solution(4034198657431611664)
XLA Ops:
  0.7 0.0 copy-start
  0.7 0.7 %copy-done = s32[8,2]{0,1:T(2,128)S(1)} copy-done((s32[8,2]{0,1:T(2,128)S(1)}, s32[8,2]{0,1:T(2,128)}, u32[]{:S(2)}) %copy-start) | copy-done | bytes 88
  1.3 25.0 %shard_map.64 = f32[2,1,128,256]{3,2,1,0:T(8,128)S(1)} custom-call(bf16[1,1,2,256,256]{4,3,2,1,0:T(8,128)(2,1)} %waves_hbm.1, bf16[1,1,2,256,256]{4,3,2,1,0:T(8,128)(2,1)} %layers_hbm.1, f32[1,2,256,256]{3,2,1,0:T(8,128)} %residual_hbm.1, s32[2,8]{1,0:T(2,128)S(1)} %bitcast.1, s32[1]{0:T(128)S(6)} %copy.8.slot, bf16[2,256,512]{2,1,0:T(8,128)(2,1)} %constant.2.clone.table_hbm), custom_call_target="tpu_custom_call" | custom-call | tf_op jit(solution)/shard_map/pallas_call | solution.py:365
  26.3 0.7 %copy.9 = f32[2,1,128,256]{3,2,1,0:T(8,128)} copy(f32[2,1,128,256]{3,2,1,0:T(8,128)S(1)} %shard_map.64) | data formatting | bytes 524288
Async XLA Ops:
  0.7 0.7 %copy-start = (s32[8,2]{0,1:T(2,128)S(1)}, s32[8,2]{0,1:T(2,128)}, u32[]{:S(2)}) copy-start(s32[8,2]{0,1:T(2,128)} %param.9) | copy-start | bytes 196

commit v7 on v6

--- a/solution.py
+++ b/solution.py
@@ -266,11 +266,14 @@
     patch_row = lax.broadcasted_iota(jnp.int32, (rows, side), 1)
     distance = strip_row - patch_row
 
-    def strip(owner):
+    def strip_part(owner, c):
         shifted = distance + owner * rows
         own_rows = onehot(shifted == top_row)
         peer_rows = onehot(shifted == peer_row)
-        return [dot(own_rows, placed[c][0]) + dot(peer_rows, placed[c][1]) for c in range(2)]
+        return dot(own_rows, placed[c][0]) + dot(peer_rows, placed[c][1])
+
+    def strip(owner):
+        return [strip_part(owner, c) for c in range(2)]
 
     def direct_copy(mask, c):
         place = mask - 1 if c == 0 else probe_count - 1
@@ -306,10 +309,10 @@
     others = range(probe_count // 2 - 1, 0, -1)
     for other in others:
         mask = 2 * other + 1
-        real, imag = strip(flip(probe, mask, probe_count))
-        pair_out[other - 1] = imag.astype(BF16)
+        owner = flip(probe, mask, probe_count)
+        pair_out[other - 1] = strip_part(owner, 1).astype(BF16)
         pair_copy(other - 1).start()
-        direct_out[mask - 1] = real.astype(BF16)
+        direct_out[mask - 1] = strip_part(owner, 0).astype(BF16)
         direct_copy(mask, 0).start()
     for other in others:
         mask = 2 * other

time: 27.2 us -> 27.2 us (level)
  no operation moved by 1% of the time
where the time goes in v7:
time: 27.2 us; the launch traced here: 27.1 us
  Pallas kernels  25 us (92%)
  local copies, waits for them, and re-layouts  1.38 us (5%)
  between operations  0.67 us (2%)
    pallas_call x1, Pallas kernels, per_device(): pl.pallas_call(functools.partial(kernel, depth_count, probe_count), out_s...  25 us
    unnamed x3, local copies, waits for them, and re-layouts  1.38 us

profile of v7, /device:TPU:0, one launch (start us, length us, event | category | flops | bytes accessed | tf_op | source)
XLA Modules:
  0.0 27.1 jit_solution(15299725687851869445)
XLA Ops:
  0.7 0.0 copy-start
  0.7 0.7 %copy-done = s32[8,2]{0,1:T(2,128)S(1)} copy-done((s32[8,2]{0,1:T(2,128)S(1)}, s32[8,2]{0,1:T(2,128)}, u32[]{:S(2)}) %copy-start) | copy-done | bytes 88
  1.3 25.0 %shard_map.64 = f32[2,1,128,256]{3,2,1,0:T(8,128)S(1)} custom-call(bf16[1,1,2,256,256]{4,3,2,1,0:T(8,128)(2,1)} %waves_hbm.1, bf16[1,1,2,256,256]{4,3,2,1,0:T(8,128)(2,1)} %layers_hbm.1, f32[1,2,256,256]{3,2,1,0:T(8,128)} %residual_hbm.1, s32[2,8]{1,0:T(2,128)S(1)} %bitcast.1, s32[1]{0:T(128)S(6)} %copy.8.slot, bf16[2,256,512]{2,1,0:T(8,128)(2,1)} %constant.2.clone.table_hbm), custom_call_target="tpu_custom_call" | custom-call | tf_op jit(solution)/shard_map/pallas_call | solution.py:368
  26.3 0.7 %copy.9 = f32[2,1,128,256]{3,2,1,0:T(8,128)} copy(f32[2,1,128,256]{3,2,1,0:T(8,128)S(1)} %shard_map.64) | data formatting | bytes 524288
Async XLA Ops:
  0.7 0.7 %copy-start = (s32[8,2]{0,1:T(2,128)S(1)}, s32[8,2]{0,1:T(2,128)}, u32[]{:S(2)}) copy-start(s32[8,2]{0,1:T(2,128)} %param.9) | copy-start | bytes 196
